TPU v7x, 256 devices: a whole 4x4x8 slice. The times are simulated.
256 devices in a mesh: dp: 8 (over z), expert: 8 (over x, core), tensor: 4 (over y).
Axes of the slice: x: 4, y: 4, z: 8, core: 2. Of those that a mesh axis runs over, the one named last changes fastest.
Arguments:
- skip_stream_entry: bfloat16 [4096, 4096], P(('dp', 'expert', 'tensor')), may hold values from -6 to 6
- question_vectors: bfloat16 [4096, 2048], P(('dp', 'expert'), 'tensor'), may hold values from -5 to 5
- fresh_lookup_vectors: bfloat16 [4096, 512], P(('dp', 'expert'), 'tensor'), may hold values from -5 to 5
- fresh_content_vectors: bfloat16 [4096, 512], P(('dp', 'expert'), 'tensor'), may hold values from -10 to 10
- stored_lookup_sheets: bfloat16 [2560, 4, 128, 128], P(('dp', 'expert'), 'tensor'), may hold values from -5 to 5
- stored_content_sheets: bfloat16 [2560, 4, 128, 128], P(('dp', 'expert'), 'tensor'), may hold values from -10 to 10
- sequence_sheet_map: int32 [1088, 8], P(('dp', 'expert')), may hold values from 0 to 39
- stored_position_counts: int32 [1088], P(('dp', 'expert')), may hold values from 2 to 1024
- attention_merge_matrix: bfloat16 [2048, 4096], P('tensor'), may hold values from -0.59765625 to 0.59765625
- premix_scale_factor: bfloat16 [4096], replicated, may hold values from 0.5 to 1.5
- chosen_specialists: int32 [4096, 2], P(('dp', 'expert', 'tensor')), may hold values from 0 to 7, all different within a row; in each aligned block of 16 rows (0 to 15, 16 to 31, ...) at most 6 rows name the same one
- selection_shares: float32 [4096, 2], P(('dp', 'expert', 'tensor')), may hold values from 0.2 to 1
- allowed_placements: int32 [8], replicated, may hold values from 2 to 3
- favored_specialist: int32 [1], replicated, may hold values from 0 to 7
- gating_matrices: bfloat16 [8, 7168, 4096], P('expert', ('dp', 'tensor')), may hold values from -0.09375 to 0.09375
- expand_matrices: bfloat16 [8, 7168, 4096], P('expert', ('dp', 'tensor')), may hold values from -0.09375 to 0.09375
- contract_matrices: bfloat16 [8, 7168, 4096], P('expert', ('dp', 'tensor')), may hold values from -0.0625 to 0.0625
Outputs:
- layer_out: bfloat16 [4096, 4096], P(('dp', 'expert', 'tensor'))
Inputs may be any that keep to these rules, and one draw needn't show every extreme that they name: `chosen_specialists`: in the 16 rows of one device no expert is named by more than 6 rows; a token names two different experts.
All inputs are finite; a program needn't handle non-finite values.
Results may differ from a plain program's by a relative error of at most 0.018.
Values may be sent and summed in bfloat16 or wider, within the bound.
A program may use at most 128 MiB of HBM per device.

v0:
```python
from functools import reduce
import math
import jax
import jax.numpy as jnp
from jax import lax
from jax.sharding import PartitionSpec as P

HD = 128
PLACEMENT_MOST = 6


def normalize(parts):
    highest = reduce(
        jnp.maximum,
        [
            jnp.max(jnp.where(visible, scores, -jnp.inf), axis=-1, keepdims=True)
            for scores, visible in parts
        ],
    )
    portions = [jnp.where(visible, jnp.exp(scores - highest), 0.0) for scores, visible in parts]
    denominator = reduce(
        jnp.add, [jnp.sum(portion, axis=-1, keepdims=True) for portion in portions]
    )
    return [(portion / denominator).astype(jnp.bfloat16) for portion in portions]


def attend(question_vectors, new_keys, new_values, key_pages, value_pages, table, spans):
    rows_all, head_count, head_width = question_vectors.shape
    kv_heads = new_keys.shape[1]
    group_size = head_count // kv_heads
    single_count = spans.shape[0] - 1
    page_count = table.shape[1]
    page_width = key_pages.shape[2]
    context = page_count * page_width
    inverse_root = 1.0 / math.sqrt(head_width)
    page_keys = key_pages[table]
    page_values = value_pages[table]
    grouped = question_vectors.reshape(rows_all, kv_heads, group_size, head_width)
    positions = jnp.arange(context, dtype=jnp.int32)
    single_q = grouped[:single_count]
    cache_dec = (
        jnp.einsum(
            "rkgh,rmkph->rkgmp",
            single_q,
            page_keys[:single_count],
            preferred_element_type=jnp.float32,
        ).reshape(single_count, kv_heads, group_size, context)
        * inverse_root
    )
    seen_dec = (positions[None, :] < spans[:single_count, None])[:, None, None, :]
    own_dec = (
        jnp.einsum(
            "rkgh,rkh->rkg", single_q, new_keys[:single_count], preferred_element_type=jnp.float32
        )[..., None]
        * inverse_root
    )
    weight_cache, weight_own = normalize(
        [(cache_dec, seen_dec), (own_dec, jnp.full(own_dec.shape, True))]
    )
    out_dec = jnp.einsum(
        "rkgmp,rmkph->rkgh",
        weight_cache.reshape(single_count, kv_heads, group_size, page_count, page_width),
        page_values[:single_count],
        preferred_element_type=jnp.float32,
    )
    out_dec = (
        out_dec
        + weight_own.astype(jnp.float32)
        * new_values[:single_count].astype(jnp.float32)[:, :, None, :]
    )
    prompt_q = grouped[single_count:]
    prompt_rows = rows_all - single_count
    cache_pro = (
        jnp.einsum(
            "rkgh,mkph->rkgmp",
            prompt_q,
            page_keys[single_count],
            preferred_element_type=jnp.float32,
        ).reshape(prompt_rows, kv_heads, group_size, context)
        * inverse_root
    )
    seen_pro = (positions < spans[single_count])[None, None, None, :]
    new_pro = (
        jnp.einsum(
            "rkgh,mkh->rkgm", prompt_q, new_keys[single_count:], preferred_element_type=jnp.float32
        )
        * inverse_root
    )
    prompt_index = jnp.arange(prompt_rows, dtype=jnp.int32)
    causal = (prompt_index[:, None] >= prompt_index[None, :])[:, None, None, :]
    weight_cpro, weight_npro = normalize([(cache_pro, seen_pro), (new_pro, causal)])
    out_pro = jnp.einsum(
        "rkgmp,mkph->rkgh",
        weight_cpro.reshape(prompt_rows, kv_heads, group_size, page_count, page_width),
        page_values[single_count],
        preferred_element_type=jnp.float32,
    )
    out_pro = out_pro + jnp.einsum(
        "rkgm,mkh->rkgh", weight_npro, new_values[single_count:], preferred_element_type=jnp.float32
    )
    joined = jnp.concatenate([out_dec, out_pro], axis=0).astype(jnp.bfloat16)
    return joined.reshape(rows_all, head_count * head_width)


def slot_table(member, ranking, keeping, slot_count):
    slot_hit = (
        ranking[:, :, None, None] == jnp.arange(slot_count, dtype=jnp.int32)[None, None, None, :]
    )
    return ((member[..., None] > 0) & keeping[:, :, None, None] & slot_hit).astype(jnp.bfloat16)


def expert_pass(send, gating_matrices, expand_matrices, contract_matrices):
    specialist_index, slot_count, model_width = send.shape
    holders = lax.axis_size("expert")
    local_count = gating_matrices.shape[0]
    arrived = lax.all_to_all(
        send.reshape(holders, local_count, slot_count, model_width),
        "expert",
        split_axis=0,
        concat_axis=0,
        tiled=True,
    )
    row_piece = lax.all_gather(arrived, ("dp", "tensor"), axis=0, tiled=True)
    gate_part = jnp.einsum(
        "qesd,efd->qesf", row_piece, gating_matrices, preferred_element_type=jnp.float32
    )
    up_part = jnp.einsum(
        "qesd,efd->qesf", row_piece, expand_matrices, preferred_element_type=jnp.float32
    )
    hidden = (jax.nn.silu(gate_part) * up_part).astype(jnp.bfloat16)
    partial_out = jnp.einsum(
        "qesf,efd->qesd", hidden, contract_matrices, preferred_element_type=jnp.float32
    ).astype(jnp.bfloat16)
    summed = lax.psum_scatter(
        lax.psum_scatter(partial_out, "dp", scatter_dimension=0, tiled=True),
        "tensor",
        scatter_dimension=0,
        tiled=True,
    )
    arrived_back = lax.all_to_all(summed, "expert", split_axis=0, concat_axis=0, tiled=True)
    return arrived_back.reshape(specialist_index, slot_count, model_width)


def local(
    skip_stream_entry,
    question_vectors,
    fresh_lookup_vectors,
    fresh_content_vectors,
    stored_lookup_sheets,
    stored_content_sheets,
    sequence_sheet_map,
    stored_position_counts,
    attention_merge_matrix,
    premix_scale_factor,
    chosen_specialists,
    selection_shares,
    allowed_placements,
    favored_specialist,
    gating_matrices,
    expand_matrices,
    contract_matrices,
):
    token_count = chosen_specialists.shape[0]
    specialist_index = allowed_placements.shape[0]
    picked = (
        chosen_specialists[:, :, None]
        == jnp.arange(specialist_index, dtype=jnp.int32)[None, None, :]
    ).astype(jnp.int32)
    flat_routes = picked.reshape(token_count * 2, specialist_index)
    busiest_specialist = favored_specialist[0]
    before = (jnp.cumsum(flat_routes, axis=0) - flat_routes).reshape(
        token_count, 2, specialist_index
    )
    ranking = jnp.sum(before * picked, axis=2)
    placement_ceiling = jnp.where(
        jnp.arange(specialist_index, dtype=jnp.int32) == busiest_specialist,
        PLACEMENT_MOST,
        allowed_placements,
    )
    keeping = ranking < jnp.sum(picked * placement_ceiling[None, None, :], axis=2)
    row_total = question_vectors.shape[0]
    heads_out = attend(
        question_vectors.reshape(row_total, -1, HD),
        fresh_lookup_vectors.reshape(row_total, -1, HD),
        fresh_content_vectors.reshape(row_total, -1, HD),
        stored_lookup_sheets,
        stored_content_sheets,
        sequence_sheet_map,
        stored_position_counts,
    )
    own_attn = lax.psum_scatter(
        jnp.dot(heads_out, attention_merge_matrix, preferred_element_type=jnp.float32).astype(
            jnp.bfloat16
        ),
        "tensor",
        scatter_dimension=0,
        tiled=True,
    ).astype(jnp.float32)
    stream = (skip_stream_entry.astype(jnp.float32) + own_attn).astype(jnp.bfloat16)
    wide = stream.astype(jnp.float32)
    squares = jnp.mean(wide * wide, axis=1, keepdims=True)
    normed = (wide * lax.rsqrt(squares + 1e-05) * premix_scale_factor.astype(jnp.float32)).astype(
        jnp.bfloat16
    )
    main_slots = PLACEMENT_MOST
    table_main = slot_table(picked, ranking, keeping, main_slots)
    send = jnp.einsum(
        "nkes,nd->esd", table_main, normed, preferred_element_type=jnp.float32
    ).astype(jnp.bfloat16)
    expert_out = expert_pass(send, gating_matrices, expand_matrices, contract_matrices)
    chosen = jnp.einsum("nkes,esd->nkd", table_main, expert_out, preferred_element_type=jnp.float32)
    mixed = jnp.sum(selection_shares[:, :, None] * chosen, axis=1)
    return (wide + mixed).astype(jnp.bfloat16)


def solution(mesh):
    placed = (
        P(("dp", "expert", "tensor"), None),
        P(("dp", "expert"), "tensor"),
        P(("dp", "expert"), "tensor"),
        P(("dp", "expert"), "tensor"),
        P(("dp", "expert"), "tensor", None, None),
        P(("dp", "expert"), "tensor", None, None),
        P(("dp", "expert"), None),
        P(("dp", "expert")),
        P("tensor", None),
        P(),
        P(("dp", "expert", "tensor"), None),
        P(("dp", "expert", "tensor"), None),
        P(),
        P(),
        P("expert", ("dp", "tensor"), None),
        P("expert", ("dp", "tensor"), None),
        P("expert", ("dp", "tensor"), None),
    )
    return jax.shard_map(
        local,
        mesh=mesh,
        in_specs=placed,
        out_specs=P(("dp", "expert", "tensor"), None),
        check_vma=False,
    )
```

profile of v0, /device:TPU:1, one launch (start us, length us, event | category | flops | bytes accessed | tf_op | source)
XLA Modules:
  0.0 416.9 jit_solution(13904441723688626765)
XLA Ops:
  7.4 1.2 slice.49
  8.7 1.2 broadcast_compare_fusion.1
  10.5 1.3 slice_bitcast_fusion.5
  12.0 1.3 slice_convert_fusion
  13.3 1.6 select_reduce_fusion.2
  14.8 8.8 %gather_fusion.1 = bf16[136,128,128]{2,1,0:T(8,128)(2,1)} fusion(bf16[40,128,128]{2,1,0:T(8,128)(2,1)} %bitcast.219, s32[1024]{0:T(1024)S(1)} %pad_clamp_fusion), kind=kCustom, calls=%fused_computation.1 | custom fusion | bytes 8913440 | tf_op jit(solution)/shard_map/gather | solution.py:37
  23.7 1.3 copy-done.1
  25.0 7.5 %gather_fusion = bf16[136,128,128]{2,1,0:T(8,128)(2,1)} fusion(bf16[40,128,128]{2,1,0:T(8,128)(2,1)S(1)} %bitcast.220, s32[1024]{0:T(1024)S(1)} %pad_clamp_fusion), kind=kCustom, calls=%fused_computation | custom fusion | bytes 8913440 | tf_op jit(solution)/shard_map/gather | solution.py:36
  33.4 1.7 select_reduce_fusion
  36.4 1.3 select_reduce_fusion.1
  38.0 1.4 slice-done.2
  40.1 1.6 convolution_convert_fusion
  43.4 24.8 %reduce-scatter.6.cloned.1.call-done = bf16[16,4096]{1,0:T(8,128)(2,1)} async-done(((bf16[64,4096]{1,0:T(8,128)(2,1)}), bf16[16,4096]{1,0:T(8,128)(2,1)}) %reduce-scatter.6.cloned.1.call-update) | async-done | bytes 131088 | tf_op jit(solution)/shard_map/reduce_scatter | solution.py:191
  68.1 1.1 fusion.53
  69.2 1.2 fusion.5
  70.6 15.7 %all_to_all.10 = bf16[8,1,6,4096]{3,2,1,0:T(8,128)(2,1)S(1)} all-to-all(bf16[8,1,6,4096]{3,2,1,0:T(8,128)(2,1)S(1)} %copy.41), channel_id=1, replica_groups=mesh['dp'=8,'expert'=8,'tensor'=4] {'expert'}, dimensions={0} | all-to-all | bytes 786432 | tf_op jit(solution)/shard_map/all_to_all | solution.py:116
  87.6 117.5 %all-gather.2.cloned.1.call-done = bf16[256,1,6,4096]{3,0,2,1:T(8,128)(2,1)} async-done(((bf16[8,1,6,4096]{3,0,2,1:T(8,128)(2,1)}), bf16[256,1,6,4096]{3,0,2,1:T(8,128)(2,1)}) %all-gather.2.cloned.1.call-update) | async-done | bytes 12582928 | tf_op jit(solution)/shard_map/all_gather | solution.py:123
  205.1 7.5 %fusion.9 = f32[256,1,6,224]{0,3,2,1:T(8,128)S(1)} fusion(bf16[1,224,4096]{2,1,0:T(8,128)(2,1)} %param.31, bf16[256,1,6,4096]{3,0,2,1:T(8,128)(2,1)} %all-gather.2.cloned.1.call-done), kind=kOutput, calls=%fused_computation.15 | convolution fusion | flops 2818572288 | bytes 15794176 | tf_op jit(solution)/shard_map/qesd,efd->qesf/dot_general | solution.py:124
  212.6 19.3 %convert_bitcast_fusion = bf16[256,1,6,4096]{3,0,2,1:T(8,128)(2,1)} fusion(bf16[1,224,4096]{2,1,0:T(8,128)(2,1)S(1)} %copy-done, bf16[1,224,4096]{2,1,0:T(8,128)(2,1)} %param.32, bf16[256,1,6,4096]{3,0,2,1:T(8,128)(2,1)} %all-gather.2.cloned.1.call-done, f32[256,1,6,224]{0,3,2,1:T(8,128)S(1)} %fusion.9), kind=kOutput, calls=%fused_computation.6 | convolution fusion | flops 5645500416 | bytes 30212096 | tf_op jit(solution)/shard_map/qesf,efd->qesd/dot_general | solution.py:131
  232.0 132.1 %reduce-scatter.8.cloned.1.call-done = bf16[32,1,6,4096]{3,0,2,1:T(8,128)(2,1)} async-done(((bf16[256,1,6,4096]{3,0,2,1:T(8,128)(2,1)}), bf16[32,1,6,4096]{3,0,2,1:T(8,128)(2,1)}) %reduce-scatter.8.cloned.1.call-update) | async-done | bytes 1572880 | tf_op jit(solution)/shard_map/reduce_scatter | solution.py:135
  364.1 2.7 copy.58
  366.8 26.2 %reduce-scatter.10.cloned.1.call-done = bf16[8,24576]{1,0:T(8,128)(2,1)} async-done(((bf16[32,24576]{1,0:T(8,128)(2,1)}), bf16[8,24576]{1,0:T(8,128)(2,1)}) %reduce-scatter.10.cloned.1.call-update) | async-done | bytes 393232
  393.0 1.2 copy.43
  394.2 15.1 %all_to_all.11 = bf16[8,1,6,4096]{3,2,1,0:T(8,128)(2,1)S(1)} all-to-all(bf16[8,1,6,4096]{3,2,1,0:T(8,128)(2,1)S(1)} %copy.43), channel_id=1, replica_groups=mesh['dp'=8,'expert'=8,'tensor'=4] {'expert'}, dimensions={0} | all-to-all | bytes 786432 | tf_op jit(solution)/shard_map/all_to_all | solution.py:140
  (90 shorter events, 8.3 us)
Async XLA Ops:
  6.5 206.1 %copy-start = (bf16[1,224,4096]{2,1,0:T(8,128)(2,1)S(1)}, bf16[1,224,4096]{2,1,0:T(8,128)(2,1)}, u32[]{:S(2)}) copy-start(bf16[1,224,4096]{2,1,0:T(8,128)(2,1)} %param.33) | copy-start | bytes 5505028
  6.5 61.6 %reduce-scatter.6.cloned.1.call-start = ((), (), s32[]{:S(2)}) async-start(), calls=%async_computation.5 | async-start | bytes 655360 | tf_op jit(solution)/shard_map/reduce_scatter | solution.py:191
  23.7 1.3 copy-start.1
  25.0 10.7 %slice-start = ((s8[4456448]{0:T(1024)(128)(4,1)}), s8[262144]{0:T(1024)(128)(4,1)S(1)}, s32[]{:S(2)}) async-start(s8[4456448]{0:T(1024)(128)(4,1)} %bitcast.215), calls=%async_computation.9 | async-start | bytes 524288
  32.5 0.8 copy-start.8
  32.5 0.8 copy-start.12
  32.6 2.6 copy-start.10
  32.6 2.9 copy-start.13
  32.6 3.1 slice-start.1
  33.4 2.7 copy-start.14
  33.4 2.8 copy-start.9
  33.4 3.0 slice-start.3
  35.7 3.6 slice-start.2
  35.7 3.6 copy-start.7
  36.4 3.8 copy-start.2
  39.3 2.5 copy-start.5
  39.3 3.8 copy-start.6
  39.3 3.8 copy-start.15
  39.4 28.8 %copy-start.3 = (bf16[16,4096]{1,0:T(8,128)(2,1)S(1)}, bf16[16,4096]{1,0:T(8,128)(2,1)}, u32[]{:S(2)}) copy-start(bf16[16,4096]{1,0:T(8,128)(2,1)} %param.17) | copy-start | bytes 393220
  41.8 163.3 %all-gather.2.cloned.1.call-start = ((), (), s32[]{:S(2)}) async-start(), calls=%async_computation.6 | async-start | bytes 12976128 | tf_op jit(solution)/shard_map/all_gather | solution.py:123
  87.4 276.7 %reduce-scatter.8.cloned.1.call-start = ((), (), s32[]{:S(2)}) async-start(), calls=%async_computation.7 | async-start | bytes 14155776 | tf_op jit(solution)/shard_map/reduce_scatter | solution.py:135
  231.9 177.3 %copy-start.11 = (f32[16,2]{0,1:T(2,128)S(1)}, f32[16,2]{0,1:T(2,128)}, u32[]{:S(2)}) copy-start(f32[16,2]{0,1:T(2,128)} %param.28) | copy-start | bytes 388
  231.9 177.7 %copy-start.4 = (bf16[16,4096]{1,0:T(8,128)(2,1)S(1)}, bf16[16,4096]{1,0:T(8,128)(2,1)}, u32[]{:S(2)}) copy-start(bf16[16,4096]{1,0:T(8,128)(2,1)} %reduce-scatter.6.cloned.1.call-done) | copy-start | bytes 393220
  231.9 161.0 %reduce-scatter.10.cloned.1.call-start = ((), (), s32[]{:S(2)}) async-start(), calls=%async_computation.8 | async-start | bytes 1966080
Sparse Core Ops, SparseCore 0:
  41.9 26.1 reduce-scatter.5
  87.5 117.5 all-gather.1
  232.0 131.9 reduce-scatter.7
  366.9 26.0 reduce-scatter.9
where the time goes:
time: 417 us
  waiting for transfers between devices  301 us (72%)
  matrix products  35.9 us (9%)
  blocking collectives  30.8 us (7%)
  local copies, waits for them, and re-layouts  29 us (7%)
  between operations  14.2 us (3%)
  other arithmetic  6.11 us (1%)
    reduce_scatter x1, waiting for transfers between devices, expert_pass(): lax.psum_scatter(partial_out, 'dp', scatter_dimension=0, tiled=True)  132 us
    all_gather x1, waiting for transfers between devices, expert_pass(): row_piece = lax.all_gather(arrived, ('dp', 'tensor'), axis=0, tiled=True)  118 us
    unnamed x5, waiting for transfers between devices  26.2 us
    reduce_scatter x1, waiting for transfers between devices, local(): lax.psum_scatter(jnp.dot(heads_out, attention_merge_matrix, preferred_ele...  24.8 us
    dot_general x1, matrix products, expert_pass(): jnp.einsum('qesf,efd->qesd', hidden, contract_matrices, preferred_element...  19.3 us
    all_to_all x1, blocking collectives, expert_pass(): lax.all_to_all(send.reshape(holders, local_count, slot_count, model_width...  15.7 us
    all_to_all x1, blocking collectives, expert_pass(): lax.all_to_all(summed, 'expert', split_axis=0, concat_axis=0, tiled=True)  15.1 us
    gather x1, local copies, waits for them, and re-layouts, attend(): page_values = value_pages[table]  8.83 us
  transfers between devices with their start and end apart: 4, of which 4 were waited for; matrix products, arithmetic and copies ran while one was open for 0% of the time, Pallas kernels for 0%

commit v1 on v0

--- a/solution.py
+++ b/solution.py
@@ -120,7 +120,12 @@
         concat_axis=0,
         tiled=True,
     )
-    row_piece = lax.all_gather(arrived, ("dp", "tensor"), axis=0, tiled=True)
+    row_piece = jnp.concatenate(
+        lax.all_to_all(
+            jnp.stack([arrived] * lax.axis_size(("dp", "tensor"))), ("dp", "tensor"), 0, 0
+        ),
+        axis=0,
+    )
     gate_part = jnp.einsum(
         "qesd,efd->qesf", row_piece, gating_matrices, preferred_element_type=jnp.float32
     )

time: 417 us -> 587 us (1.41)
  blocking collectives: 30.8 us -> 312 us
  waiting for transfers between devices: 301 us -> 183 us
  local copies, waits for them, and re-layouts: 29 us -> 38.9 us
    all_to_all x0 -> x1, blocking collectives: none -> 281 us  [expert_pass(): lax.all_to_all(jnp.stack([arrived] * lax.axis_size(('dp', 'tensor'))), ('...]
    all_gather x1 -> x0, waiting for transfers between devices: 118 us -> none  [expert_pass(): row_piece = lax.all_gather(arrived, ('dp', 'tensor'), axis=0, tiled=True)]
    another operation x2 -> x3, local copies, waits for them, and re-layouts: 0.03 us -> 6.18 us  [the longest x1 6.16 us: expert_pass(): jnp.stack([arrived] * lax.axis_size(('dp', 'tensor')))]
    unnamed x5 -> x4, waiting for transfers between devices: 26.2 us -> 26.2 us
  transfers between devices with their start and end apart: 4 -> 3, of which waited for: 4 -> 3; matrix products, arithmetic and copies ran while one was open for 0% -> 0% of each run, Pallas kernels for 0% -> 0%
where the time goes in v1:
time: 587 us
  blocking collectives  312 us (53%)
  waiting for transfers between devices  183 us (31%)
  local copies, waits for them, and re-layouts  38.9 us (7%)
  matrix products  32.4 us (6%)
  between operations  14.1 us (2%)
  other arithmetic  6.11 us (1%)
    all_to_all x1, blocking collectives, expert_pass(): lax.all_to_all(jnp.stack([arrived] * lax.axis_size(('dp', 'tensor'))), ('...  281 us
    reduce_scatter x1, waiting for transfers between devices, expert_pass(): lax.psum_scatter(partial_out, 'dp', scatter_dimension=0, tiled=True)  132 us
    unnamed x4, waiting for transfers between devices  26.2 us
    reduce_scatter x1, waiting for transfers between devices, local(): lax.psum_scatter(jnp.dot(heads_out, attention_merge_matrix, preferred_ele...  24.8 us
    dot_general x1, matrix products, expert_pass(): jnp.einsum('qesf,efd->qesd', hidden, contract_matrices, preferred_element...  19.4 us
    all_to_all x1, blocking collectives, expert_pass(): lax.all_to_all(send.reshape(holders, local_count, slot_count, model_width...  15.7 us
    all_to_all x1, blocking collectives, expert_pass(): lax.all_to_all(summed, 'expert', split_axis=0, concat_axis=0, tiled=True)  15 us
  transfers between devices with their start and end apart: 3, of which 3 were waited for; matrix products, arithmetic and copies ran while one was open for 0% of the time, Pallas kernels for 0%

profile of v1, /device:TPU:1, one launch (start us, length us, event | category | flops | bytes accessed | tf_op | source)
XLA Modules:
  0.0 586.9 jit_solution(1557035913576616416)
XLA Ops:
  7.4 1.2 slice.49
  10.5 1.3 slice_bitcast_fusion.5
  12.0 1.3 slice_convert_fusion
  13.3 1.6 select_reduce_fusion.2
  14.8 8.8 %gather_fusion.1 = bf16[136,128,128]{2,1,0:T(8,128)(2,1)} fusion(bf16[40,128,128]{2,1,0:T(8,128)(2,1)} %bitcast.220, s32[1024]{0:T(1024)S(1)} %pad_clamp_fusion), kind=kCustom, calls=%fused_computation.1 | custom fusion | bytes 8913440 | tf_op jit(solution)/shard_map/gather | solution.py:37
  23.7 1.3 copy-done.1
  25.0 7.5 %gather_fusion = bf16[136,128,128]{2,1,0:T(8,128)(2,1)} fusion(bf16[40,128,128]{2,1,0:T(8,128)(2,1)S(1)} %bitcast.221, s32[1024]{0:T(1024)S(1)} %pad_clamp_fusion), kind=kCustom, calls=%fused_computation | custom fusion | bytes 8913440 | tf_op jit(solution)/shard_map/gather | solution.py:36
  33.4 1.7 select_reduce_fusion
  36.4 1.3 select_reduce_fusion.1
  38.0 1.4 slice-done.2
  40.1 1.6 convolution_convert_fusion
  43.4 24.8 %reduce-scatter.6.cloned.1.call-done = bf16[16,4096]{1,0:T(8,128)(2,1)} async-done(((bf16[64,4096]{1,0:T(8,128)(2,1)}), bf16[16,4096]{1,0:T(8,128)(2,1)}) %reduce-scatter.6.cloned.1.call-update) | async-done | bytes 131088 | tf_op jit(solution)/shard_map/reduce_scatter | solution.py:196
  69.2 1.2 fusion.7
  70.6 15.7 %all_to_all.18 = bf16[8,1,6,4096]{3,2,1,0:T(8,128)(2,1)S(1)} all-to-all(bf16[8,1,6,4096]{3,2,1,0:T(8,128)(2,1)S(1)} %copy.41), channel_id=1, replica_groups=mesh['dp'=8,'expert'=8,'tensor'=4] {'expert'}, dimensions={0} | all-to-all | bytes 786432 | tf_op jit(solution)/shard_map/all_to_all | solution.py:116
  86.6 6.2 %stack.2 = bf16[32,8,1,6,4096]{4,1,3,2,0:T(8,128)(2,1)} broadcast(bf16[8,6,4096]{2,0,1:T(8,128)(2,1)S(1)} %copy.42), dimensions={1,3,4} | broadcast | bytes 12976128 | tf_op jit(solution)/shard_map/stack | solution.py:125
  92.8 281.1 %all_to_all.19 = bf16[32,8,1,6,4096]{4,1,3,2,0:T(8,128)(2,1)S(1)} all-to-all(bf16[32,8,1,6,4096]{4,1,3,2,0:T(8,128)(2,1)} %stack.2), channel_id=1, replica_groups=mesh['dp'=8,'expert'=8,'tensor'=4] {'dp','tensor'}, dimensions={0} | all-to-all | bytes 25165824 | tf_op jit(solution)/shard_map/all_to_all | solution.py:124
  373.8 4.5 copy-done.2
  378.3 3.8 fusion.11
  382.1 19.4 %convert_bitcast_fusion = bf16[256,1,6,4096]{3,0,2,1:T(8,128)(2,1)} fusion(bf16[1,224,4096]{2,1,0:T(8,128)(2,1)S(1)} %copy-done, bf16[1,224,4096]{2,1,0:T(8,128)(2,1)} %param.32, bf16[32,8,1,6,4096]{4,1,3,2,0:T(8,128)(2,1)} %copy-done.2, f32[256,1,6,224]{0,3,2,1:T(8,128)S(1)} %fusion.11), kind=kOutput, calls=%fused_computation.6 | convolution fusion | flops 5645500416 | bytes 30212096 | tf_op jit(solution)/shard_map/qesf,efd->qesd/dot_general | solution.py:136
  401.7 132.5 %reduce-scatter.8.cloned.1.call-done = bf16[32,1,6,4096]{3,0,2,1:T(8,128)(2,1)} async-done(((bf16[256,1,6,4096]{3,0,2,1:T(8,128)(2,1)}), bf16[32,1,6,4096]{3,0,2,1:T(8,128)(2,1)}) %reduce-scatter.8.cloned.1.call-update) | async-done | bytes 1572880 | tf_op jit(solution)/shard_map/reduce_scatter | solution.py:140
  534.1 2.7 copy.59
  536.8 26.1 %reduce-scatter.10.cloned.1.call-done = bf16[8,24576]{1,0:T(8,128)(2,1)} async-done(((bf16[32,24576]{1,0:T(8,128)(2,1)}), bf16[8,24576]{1,0:T(8,128)(2,1)}) %reduce-scatter.10.cloned.1.call-update) | async-done | bytes 393232
  563.0 1.2 copy.44
  564.2 15.0 %all_to_all.20 = bf16[8,1,6,4096]{3,2,1,0:T(8,128)(2,1)S(1)} all-to-all(bf16[8,1,6,4096]{3,2,1,0:T(8,128)(2,1)S(1)} %copy.44), channel_id=1, replica_groups=mesh['dp'=8,'expert'=8,'tensor'=4] {'expert'}, dimensions={0} | all-to-all | bytes 786432 | tf_op jit(solution)/shard_map/all_to_all | solution.py:145
  (93 shorter events, 9.5 us)
Async XLA Ops:
  6.5 375.6 %copy-start = (bf16[1,224,4096]{2,1,0:T(8,128)(2,1)S(1)}, bf16[1,224,4096]{2,1,0:T(8,128)(2,1)}, u32[]{:S(2)}) copy-start(bf16[1,224,4096]{2,1,0:T(8,128)(2,1)} %param.33) | copy-start | bytes 5505028
  6.5 61.6 %reduce-scatter.6.cloned.1.call-start = ((), (), s32[]{:S(2)}) async-start(), calls=%async_computation.6 | async-start | bytes 655360 | tf_op jit(solution)/shard_map/reduce_scatter | solution.py:196
  23.7 1.3 copy-start.1
  25.0 10.7 %slice-start = ((s8[4456448]{0:T(1024)(128)(4,1)}), s8[262144]{0:T(1024)(128)(4,1)S(1)}, s32[]{:S(2)}) async-start(s8[4456448]{0:T(1024)(128)(4,1)} %bitcast.216), calls=%async_computation.9 | async-start | bytes 524288
  32.5 0.8 copy-start.9
  32.6 2.6 copy-start.11
  32.6 2.9 copy-start.14
  32.6 3.1 slice-start.1
  33.4 2.7 copy-start.15
  33.4 2.8 copy-start.10
  33.4 3.0 slice-start.3
  35.7 3.6 slice-start.2
  35.7 3.6 copy-start.8
  36.4 3.8 copy-start.3
  39.3 2.5 copy-start.6
  39.3 3.8 copy-start.7
  39.3 3.8 copy-start.17
  39.4 28.8 %copy-start.4 = (bf16[16,4096]{1,0:T(8,128)(2,1)S(1)}, bf16[16,4096]{1,0:T(8,128)(2,1)}, u32[]{:S(2)}) copy-start(bf16[16,4096]{1,0:T(8,128)(2,1)} %param.17) | copy-start | bytes 393220
  41.8 492.3 %reduce-scatter.8.cloned.1.call-start = ((), (), s32[]{:S(2)}) async-start(), calls=%async_computation.7 | async-start | bytes 14155776 | tf_op jit(solution)/shard_map/reduce_scatter | solution.py:140
  92.8 285.5 %copy-start.16 = (bf16[1,224,4096]{2,1,0:T(8,128)(2,1)S(1)}, bf16[1,224,4096]{2,1,0:T(8,128)(2,1)}, u32[]{:S(2)}) copy-start(bf16[1,224,4096]{2,1,0:T(8,128)(2,1)} %param.31) | copy-start | bytes 5505028
  373.8 4.5 copy-start.2
  401.6 177.7 %copy-start.12 = (f32[16,2]{0,1:T(2,128)S(1)}, f32[16,2]{0,1:T(2,128)}, u32[]{:S(2)}) copy-start(f32[16,2]{0,1:T(2,128)} %param.28) | copy-start | bytes 388
  401.6 178.0 %copy-start.5 = (bf16[16,4096]{1,0:T(8,128)(2,1)S(1)}, bf16[16,4096]{1,0:T(8,128)(2,1)}, u32[]{:S(2)}) copy-start(bf16[16,4096]{1,0:T(8,128)(2,1)} %reduce-scatter.6.cloned.1.call-done) | copy-start | bytes 393220
  401.6 161.4 %reduce-scatter.10.cloned.1.call-start = ((), (), s32[]{:S(2)}) async-start(), calls=%async_computation.8 | async-start | bytes 1966080
  (1 other events, 0.8 us)
Sparse Core Ops, SparseCore 0:
  41.9 26.1 reduce-scatter.5
  401.7 132.3 reduce-scatter.7
  537.0 25.9 reduce-scatter.9
